TPU v7x, 128 devices: a whole 4x4x4 slice. The times are simulated.
128 devices in a mesh: wide: 16 (over x_lo, y, core), narrow: 8 (over x_hi, z).
Axes of the slice: x: 4 (x_hi: 2, x_lo: 2; x = x_hi * 2 + x_lo), y: 4, z: 4, core: 2. Of those that a mesh axis runs over, the one named last changes fastest.
Arguments:
- inputs: bfloat16 [1792, 16384], P('wide', 'narrow'), may hold values from -6 to 6
- grad_out: bfloat16 [1792, 53248], P('narrow', 'wide'), may hold values from -6 to 6
- w_base: bfloat16 [16384, 53248], P('narrow', 'wide'), may hold values from -0.046875 to 0.046875
- adapter_down_matrix: bfloat16 [16384, 256], P('narrow'), may hold values from -0.046875 to 0.046875
- b_factor: bfloat16 [256, 53248], P(None, 'wide'), may hold values from -0.375 to 0.375
Outputs:
- input_gradient: bfloat16 [1792, 16384], P('wide', 'narrow')
- grad_a: float32 [16384, 256], P('narrow')
- grad_b: float32 [256, 53248], P(None, 'wide')
All inputs are finite; a program needn't handle non-finite values.
Results may differ from a plain program's by a relative error of at most 0.0046.
Values may be sent and summed in bfloat16 or wider, within the bound.
A program may use at most 128 MiB of HBM per device.

v0:
```python
import jax
import jax.numpy as jnp
from jax import lax
from jax.sharding import PartitionSpec as P

adapter_scale = 2.0


def contract_trailing_axis(left, right):
    return lax.dot_general(
        left, right, (((1,), (1,)), ((), ())), preferred_element_type=jnp.float32
    )


def contract_first(left, right):
    return lax.dot_general(
        left, right, (((0,), (0,)), ((), ())), preferred_element_type=jnp.float32
    )


def shards(inputs, grad_out, w_base, adapter_down_matrix, b_factor):
    width_in = w_base.shape[0]
    own_rows = grad_out.shape[0]
    owner_rows = inputs.shape[0]
    token_total_count = owner_rows * lax.axis_size("wide")
    adapter_matrix = adapter_scale / token_total_count
    block_rows = lax.all_gather(grad_out, "narrow", axis=0, tiled=True)
    base_part = contract_trailing_axis(block_rows, w_base)
    low_part = contract_trailing_axis(block_rows, b_factor)
    stacked = jnp.concatenate([base_part, low_part], axis=1)
    summed = lax.psum_scatter(stacked, "wide", scatter_dimension=0, tiled=True)
    frozen_weight_rows = summed[:, :width_in]
    low_rank_gradient = summed[:, width_in:].astype(jnp.bfloat16)
    input_gradient = (
        frozen_weight_rows
        + adapter_scale * contract_trailing_axis(low_rank_gradient, adapter_down_matrix)
    ).astype(jnp.bfloat16)
    grad_a = lax.psum(adapter_matrix * contract_first(inputs, low_rank_gradient), "wide")
    low_part = jnp.dot(inputs, adapter_down_matrix, preferred_element_type=jnp.float32)
    low_act = lax.psum(low_part, "narrow").astype(jnp.bfloat16)
    low_all = lax.all_gather(low_act, "wide", axis=0, tiled=True)
    start_row = lax.axis_index("narrow") * own_rows
    low_mine = lax.dynamic_slice_in_dim(low_all, start_row, own_rows, 0)
    grad_b = lax.psum(adapter_matrix * contract_first(low_mine, grad_out), "narrow")
    return (input_gradient, grad_a, grad_b)


def solution(mesh):
    return jax.shard_map(
        shards,
        mesh=mesh,
        in_specs=(
            P("wide", "narrow"),
            P("narrow", "wide"),
            P("narrow", "wide"),
            P("narrow", None),
            P(None, "wide"),
        ),
        out_specs=(P("wide", "narrow"), P("narrow", None), P(None, "wide")),
        check_vma=False,
    )
```

profile of v0, /device:TPU:2, one launch (start us, length us, event | category | flops | bytes accessed | tf_op | source)
XLA Modules:
  0.0 534.1 jit_solution(3243102436500479245)
XLA Ops:
  7.2 0.0 copy-start
  7.2 0.0 all-gather.2.cloned.1.call-start
  7.2 0.7 all-gather.2.cloned.1.call-update
  7.9 0.0 reduce-scatter.2.cloned.1.call-start
  8.0 142.5 %all-gather.2.cloned.1.call-done = bf16[1792,3328]{1,0:T(8,128)(2,1)} async-done(((bf16[224,3328]{1,0:T(8,128)(2,1)}), bf16[1792,3328]{1,0:T(8,128)(2,1)}) %all-gather.2.cloned.1.call-update) | async-done | bytes 11927568 | tf_op jit(solution)/shard_map/all_gather | solution.py:27
  150.4 0.0 copy-done
  150.5 6.2 %fusion.6 = f32[1792,256]{1,0:T(8,128)S(1)} fusion(bf16[1792,3328]{1,0:T(8,128)(2,1)} %all-gather.2.cloned.1.call-done, bf16[256,3328]{1,0:T(8,128)(2,1)S(1)} %copy-done), kind=kOutput, calls=%fused_computation.11 | convolution fusion | flops 3053453312 | bytes 15466496 | tf_op jit(solution)/shard_map/dot_general | solution.py:10
  156.7 33.6 %fusion.5 = f32[1792,2048]{1,0:T(8,128)S(1)} fusion(bf16[1792,3328]{1,0:T(8,128)(2,1)} %all-gather.2.cloned.1.call-done, bf16[2048,3328]{1,0:T(8,128)(2,1)} %param.7), kind=kOutput, calls=%fused_computation.10 | convolution fusion | flops 24427626496 | bytes 40239104 | tf_op jit(solution)/shard_map/dot_general | solution.py:10
  190.3 6.0 %pad_maximum_fusion = f32[1792,2304]{1,0:T(8,128)} fusion(f32[1792,256]{1,0:T(8,128)S(1)} %fusion.6, f32[1792,2048]{1,0:T(8,128)S(1)} %fusion.5), kind=kLoop, calls=%fused_computation | loop fusion | flops 4128768 | bytes 33030144 | tf_op jit(solution)/shard_map/concatenate | solution.py:30
  196.3 0.0 copy-start.4
  196.3 0.0 reduce-scatter.2.cloned.1.call-update
  196.3 0.0 copy-start.3
  196.3 0.0 copy-start.2
  196.4 0.0 all-reduce.3.cloned.1.call-start
  196.4 94.8 %reduce-scatter.2.cloned.1.call-done = f32[112,2304]{1,0:T(8,128)} async-done(((f32[1792,2304]{1,0:T(8,128)}), f32[112,2304]{1,0:T(8,128)}) %reduce-scatter.2.cloned.1.call-update) | async-done | bytes 1032208 | tf_op jit(solution)/shard_map/reduce_scatter | solution.py:31
  291.2 0.0 copy-done.4
  291.2 2.7 fusion
  293.9 0.0 all-reduce.3.cloned.1.call-update
  293.9 0.0 all-reduce.5.cloned.1.call-start
  294.0 0.0 copy-done.3
  294.0 0.3 fusion.7
  294.3 43.0 %psum.22 = bf16[112,256]{1,0:T(8,128)(2,1)S(1)} all-reduce(f32[112,256]{1,0:T(8,128)S(1)} %fusion.7), channel_id=1, replica_groups=mesh['wide'=16,'narrow'=8] {'narrow'}, use_global_device_ids=true, to_apply=%region_2.0 | all-reduce | flops 28672 | bytes 172032 | tf_op jit(solution)/shard_map/psum | solution.py:40
  337.3 19.6 %all_gather.7 = bf16[1792,256]{1,0:T(8,128)(2,1)S(1)} all-gather(bf16[112,256]{1,0:T(8,128)(2,1)S(1)} %psum.22), channel_id=1, replica_groups=mesh['wide'=16,'narrow'=8] {'wide'}, dimensions={0}, use_global_device_ids=true | all-gather | bytes 974848 | tf_op jit(solution)/shard_map/all_gather | solution.py:41
  356.9 0.0 copy-done.2
  356.9 2.4 convolution_multiply_fusion
  359.3 0.0 all-reduce.5.cloned.1.call-update
  359.4 2.5 fusion.2
  361.8 56.8 %all-reduce.3.cloned.1.call-done = f32[2048,256]{0,1:T(8,128)} async-done(((f32[2048,256]{0,1:T(8,128)}), f32[2048,256]{0,1:T(8,128)}) %all-reduce.3.cloned.1.call-update) | async-done | bytes 2097168 | tf_op jit(solution)/shard_map/psum | solution.py:38
  418.6 0.0 copy-start.1
  418.6 3.0 copy.9
  421.6 102.0 %all-reduce.5.cloned.1.call-done = f32[256,3328]{1,0:T(8,128)} async-done(((f32[256,3328]{1,0:T(8,128)}), f32[256,3328]{1,0:T(8,128)}) %all-reduce.5.cloned.1.call-update) | async-done | bytes 3407888 | tf_op jit(solution)/shard_map/psum | solution.py:44
  523.7 3.9 copy.13
  527.6 0.0 copy-done.1
Async XLA Ops:
  7.2 143.3 %copy-start = (bf16[256,3328]{1,0:T(8,128)(2,1)S(1)}, bf16[256,3328]{1,0:T(8,128)(2,1)}, u32[]{:S(2)}) copy-start(bf16[256,3328]{1,0:T(8,128)(2,1)} %param.9) | copy-start | bytes 5111812
  7.2 143.3 %all-gather.2.cloned.1.call-start = ((), (), s32[]{:S(2)}) async-start(), calls=%async_computation.1 | async-start | bytes 13418496 | tf_op jit(solution)/shard_map/all_gather | solution.py:27
  7.9 283.3 %reduce-scatter.2.cloned.1.call-start = ((), (), s32[]{:S(2)}) async-start(), calls=%async_computation.2 | async-start | bytes 17547264 | tf_op jit(solution)/shard_map/reduce_scatter | solution.py:31
  196.3 94.9 %copy-start.4 = (bf16[112,2048]{1,0:T(8,128)(2,1)S(1)}, bf16[112,2048]{1,0:T(8,128)(2,1)}, u32[]{:S(2)}) copy-start(bf16[112,2048]{1,0:T(8,128)(2,1)} %param.5) | copy-start | bytes 1376260
  196.3 97.7 %copy-start.3 = (bf16[2048,256]{1,0:T(8,128)(2,1)S(1)}, bf16[2048,256]{1,0:T(8,128)(2,1)}, u32[]{:S(2)}) copy-start(bf16[2048,256]{1,0:T(8,128)(2,1)} %param.8) | copy-start | bytes 3145732
  196.3 160.6 %copy-start.2 = (bf16[224,3328]{1,0:T(8,128)(2,1)S(1)}, bf16[224,3328]{1,0:T(8,128)(2,1)}, u32[]{:S(2)}) copy-start(bf16[224,3328]{1,0:T(8,128)(2,1)} %param.6) | copy-start | bytes 4472836
  196.4 222.3 %all-reduce.3.cloned.1.call-start = ((), (), s32[]{:S(2)}) async-start(), calls=%async_computation.3 | async-start | bytes 4194304 | tf_op jit(solution)/shard_map/psum | solution.py:38
  293.9 229.7 %all-reduce.5.cloned.1.call-start = ((), (), s32[]{:S(2)}) async-start(), calls=%async_computation.4 | async-start | bytes 6815744 | tf_op jit(solution)/shard_map/psum | solution.py:44
  418.6 109.0 %copy-start.1 = (bf16[256,3328]{1,0:T(8,128)(2,1)S(1)}, bf16[256,3328]{1,0:T(8,128)(2,1)}, u32[]{:S(2)}) copy-start(bf16[256,3328]{1,0:T(8,128)(2,1)} %param.9) | copy-start | bytes 5111812
Sparse Core Ops, SparseCore 0:
  10.3 140.1 all-gather.1
  196.4 94.7 reduce-scatter.1
  294.3 124.2 all-reduce.2
  421.6 102.0 all-reduce.4
where the time goes:
time: 535 us; the launch traced here: 534 us
  waiting for transfers between devices  397 us (74%)
  blocking collectives  62.6 us (12%)
  matrix products  47.7 us (9%)
  between operations  13.8 us (3%)
  local copies, waits for them, and re-layouts  6.97 us (1%)
  other arithmetic  5.99 us (1%)
    all_gather x1, waiting for transfers between devices, shards(): block_rows = lax.all_gather(grad_out, 'narrow', axis=0, tiled=True)  142 us
    psum x1, waiting for transfers between devices, shards(): lax.psum(adapter_matrix * contract_first(low_mine, grad_out), 'narrow')  102 us
    reduce_scatter x1, waiting for transfers between devices, shards(): summed = lax.psum_scatter(stacked, 'wide', scatter_dimension=0, tiled=True)  94.8 us
    psum x1, waiting for transfers between devices, shards(): lax.psum(adapter_matrix * contract_first(inputs, low_rank_gradient), 'wide')  56.8 us
    psum x1, blocking collectives, shards(): low_act = lax.psum(low_part, 'narrow').astype(jnp.bfloat16)  43 us
    dot_general x3, matrix products, contract_trailing_axis(): lax.dot_general(left, right, (((1,), (1,)), ((), ())), preferred_element_...  42.3 us
    all_gather x1, blocking collectives, shards(): low_all = lax.all_gather(low_act, 'wide', axis=0, tiled=True)  19.6 us
  transfers between devices with their start and end apart: 4, of which 4 were waited for; matrix products, arithmetic and copies ran while one was open for 2% of the time, Pallas kernels for 0%

commit v1 on v0

v1 whole, which is shorter than its diff:
```python
import jax
import jax.numpy as jnp
from jax import lax
from jax.experimental import pallas as pl
from jax.experimental.pallas import tpu as pltpu
from jax.sharding import PartitionSpec as P

ADAPTER_SCALE = 2.0
ROWS = 112
F_LOCAL = 3328
D_LOCAL = 2048
R = 256
TILE = 256
TILES = (R + D_LOCAL) // TILE
PARTS = 3
PER_PART = TILES // PARTS
STEPS = 8
MESH = pl.DeviceIdType.MESH
BF16 = jnp.bfloat16
F32 = jnp.float32

ORDER = (
    ((0, 0), (0, 1), (1, 0), (0, 3), (1, 1), (0, 2), (1, 2), (1, 3)),
    ((0, 0), (0, 3), (0, 1), (0, 2), (1, 3), (1, 0), (1, 2), (1, 1)),
)


def dot_nt(a, b):
    return lax.dot_general(a, b, (((1,), (1,)), ((), ())), preferred_element_type=F32)


def dot_nn(a, b):
    return lax.dot_general(a, b, (((1,), (0,)), ((), ())), preferred_element_type=F32)


def pick(index, values):
    if isinstance(index, int):
        return values[index]
    out = index * 0 + values[0]
    for i, value in enumerate(values[1:], 1):
        out = out + (index == i).astype(jnp.int32) * (value - values[0])
    return out


def kernel(
    x_hbm, g_hbm, w_hbm, a_hbm, b_hbm,
    ig_ref, ga_ref, gb_ref,
    g, w, a, xs_all, part_send, part_recv, mine, y_recv, y_own, x_send, x_recv,
    lp, l1, l2s, l2r, lo, la, la_t, lg, lg_t,
    ld_sem, g_ss, g_rs, c_ss, c_rs, y_ss, y_rs, x_ss, x_rs,
    in_ss, in_rs, la_ss, la_rs, lg_ss, lg_rs, l1_ss, l1_rs, l2_ss, l2_rs, l3_ss, l3_rs,
):
    wi = lax.axis_index("wide")
    ni = lax.axis_index("narrow")
    xl, y, c = wi // 8, (wi // 2) % 4, wi % 2
    xh, z = ni // 4, ni % 4

    def wide_id(xl_, y_, c_):
        return (xl_ * 4 + y_) * 2 + c_

    def ring(v, k):
        return (v + k) % 4

    def wide_dev(xl_, y_, c_):
        return (wide_id(xl_, y_, c_), ni)

    partner = wide_dev(xl, y, 1 - c)
    x_pair = wide_dev(1 - xl, y, c)
    x_cross = (wi, (1 - xh) * 4 + z)
    z_next = (wi, xh * 4 + ring(z, 1))
    z_prev = (wi, xh * 4 + ring(z, 3))

    def send(src, dst, ss, rs, dev):
        cp = pltpu.make_async_remote_copy(
            src_ref=src, dst_ref=dst, send_sem=ss, recv_sem=rs, device_id=dev, device_id_type=MESH
        )
        cp.start()
        return cp

    def arrived(dst, rs, ss):
        pltpu.make_async_remote_copy(
            src_ref=dst, dst_ref=dst, send_sem=ss, recv_sem=rs, device_id=partner, device_id_type=MESH
        ).wait_recv()

    def sent(src, ss, rs):
        pltpu.make_async_remote_copy(
            src_ref=src, dst_ref=src, send_sem=ss, recv_sem=rs, device_id=partner, device_id_type=MESH
        ).wait_send()

    loads = [
        pltpu.make_async_copy(x_hbm, xs_all.at[wi], ld_sem.at[0]),
        pltpu.make_async_copy(a_hbm, a, ld_sem.at[1]),
        pltpu.make_async_copy(g_hbm.at[pl.ds(0, ROWS)], g.at[0], ld_sem.at[2]),
        pltpu.make_async_copy(g_hbm.at[pl.ds(ROWS, ROWS)], g.at[1], ld_sem.at[3]),
        pltpu.make_async_copy(b_hbm, w.at[pl.ds(0, R)], ld_sem.at[4]),
        pltpu.make_async_copy(w_hbm, w.at[pl.ds(R, D_LOCAL)], ld_sem.at[5]),
    ]
    for cp in loads:
        cp.start()

    barrier = pltpu.get_barrier_semaphore()
    peers = [(wi, xh * 4 + ring(z, k)) for k in (1, 2, 3)] + [x_cross, partner]
    for dx in (0, 1):
        for k in range(4):
            if dx or k:
                peers.append(wide_dev(xl if dx == 0 else 1 - xl, ring(y, k), c))
    for dev in peers:
        pl.semaphore_signal(barrier, inc=1, device_id=dev, device_id_type=MESH)
    pl.semaphore_wait(barrier, len(peers))

    g_sends = []

    def g_send(src, dst, dev):
        slot = dst[0] * 2 + dst[1]
        sem = len(g_sends)
        send(src, g.at[slot], g_ss.at[sem], g_rs.at[slot], dev)
        g_sends.append(sem)

    def g_wait(step, kind):
        slot = step * 2 + kind
        arrived(g.at[slot], g_rs.at[slot], g_ss.at[0])

    def unit(step, kind):
        return g.at[step * 2 + kind]

    own0, own1 = g_hbm.at[pl.ds(0, ROWS)], g_hbm.at[pl.ds(ROWS, ROWS)]
    g_send(own0, (2, 0), x_cross)
    g_send(own1, (1, 1), z_next)
    g_send(own0, (1, 0), z_prev)

    def spread_own(buf, ss, rs):
        me = buf.at[wi]
        send(me, me, ss.at[0], rs.at[wi], x_pair)
        for k in (1, 3, 2):
            send(me, me, ss.at[k], rs.at[wi], wide_dev(xl, ring(y, k), c))
        send(me, me, ss.at[4], rs.at[wi], partner)

    def spread_pair(buf, ss, rs):
        other = wide_id(1 - xl, y, c)
        blk = buf.at[other]
        arrived(blk, rs.at[other], ss.at[0])
        for i, k in enumerate((1, 3, 2)):
            send(blk, blk, ss.at[5 + i], rs.at[other], wide_dev(xl, ring(y, k), c))
        send(blk, blk, ss.at[8], rs.at[other], partner)

    def spread_core(buf, ss, rs):
        i = 9
        for xl_ in (xl, 1 - xl):
            for k in (1, 3, 2):
                other = wide_id(xl_, ring(y, k), c)
                blk = buf.at[other]
                arrived(blk, rs.at[other], ss.at[0])
                send(blk, blk, ss.at[i], rs.at[other], partner)
                i += 1

    def spread_end(buf, ss, rs):
        for xl_ in (0, 1):
            for y_ in range(4):
                other = wide_id(xl_, y_, 1 - c)
                arrived(buf.at[other], rs.at[other], ss.at[0])

    def spread_sent(buf, ss, rs):
        for i in range(15):
            sent(buf.at[wi], ss.at[i], rs.at[wi])

    loads[0].wait()
    spread_own(xs_all, in_ss, in_rs)

    loads[1].wait()
    low = dot_nn(xs_all[wi], a[...])
    for rh in (0, 1):
        for ch in (0, 1):
            lp[rh * 2 + ch] = low[rh * 56:rh * 56 + 56, ch * 128:ch * 128 + 128]

    def low_stage1():
        for k in (1, 3, 2):
            q = ring(z, k)
            send(lp.at[q], l1.at[3 - k], l1_ss.at[k - 1], l1_rs.at[3 - k], (wi, xh * 4 + q))

    def low_stage2():
        for k in range(3):
            arrived(l1.at[k], l1_rs.at[k], l1_ss.at[k])
        l2s[...] = lp[z] + l1[0] + l1[1] + l1[2]
        send(l2s, l2r, l2_ss, l2_rs, x_cross)

    def low_stage3():
        arrived(l2r, l2_rs, l2_ss)
        lo[z] = l2s[...] + l2r[...]
        for k in (1, 3, 2):
            send(lo.at[z], lo.at[z], l3_ss.at[k - 1], l3_rs.at[z], (wi, xh * 4 + ring(z, k)))

    def low_stage4():
        for k in (1, 2, 3):
            q = ring(z, k)
            arrived(lo.at[q], l3_rs.at[q], l3_ss.at[k - 1])
        top = jnp.concatenate([lo[0], lo[1]], axis=1)
        bottom = jnp.concatenate([lo[2], lo[3]], axis=1)
        la[wi] = jnp.concatenate([top, bottom], axis=0).astype(BF16)
        spread_own(la, la_ss, la_rs)

    low_stage1()
    g_send(own0, (3, 0), z_next)
    g_send(own1, (2, 1), z_prev)

    for cp in loads[2:]:
        cp.wait()

    def owner(step):
        flip, dz = (
            pick(step, [t[i] for t in ORDER[0]]) * (1 - c) + pick(step, [t[i] for t in ORDER[1]]) * c
            for i in (0, 1)
        )
        return (xh + flip) % 2, ring(z, dz)

    def tiles(part):
        return pl.ds(part * PER_PART, PER_PART)

    def send_part(step, part):
        send(part_send.at[step, tiles(part)], part_recv.at[step, tiles(part)],
             c_ss.at[step, part], c_rs.at[step, part], partner)

    def join_cores(step, part):
        xl_n, y_n = owner(step)
        ref = part_recv.at[step, tiles(part)]
        arrived(ref, c_rs.at[step, part], c_ss.at[step, part])

        @pl.when(y_n == y)
        def _():
            for i in range(PER_PART):
                t = part * PER_PART + i
                y_own[xl_n, t] = mine[step % 2, t] + part_recv[step, t].astype(F32)

        @pl.when(y_n != y)
        def _():
            for i in range(PER_PART):
                t = part * PER_PART + i
                part_recv[step, t] = (mine[step % 2, t] + part_recv[step, t].astype(F32)).astype(BF16)
            r = (y - y_n + 4) % 4 - 1
            send(ref, y_recv.at[r, xl_n, tiles(part)], y_ss.at[step, part], y_rs.at[r, xl_n, part],
                 wide_dev(xl, y_n, c))

    def join_y(step, part):
        xl_n, y_n = owner(step)

        @pl.when(y_n == y)
        def _():
            for r in range(3):
                arrived(y_recv.at[r, xl_n, tiles(part)], y_rs.at[r, xl_n, part], x_ss.at[part])

            @pl.when(xl_n == xl)
            def _():
                for i in range(PER_PART):
                    t = part * PER_PART + i
                    y_own[xl_n, t] += (y_recv[0, xl_n, t].astype(F32) + y_recv[1, xl_n, t].astype(F32)
                                       + y_recv[2, xl_n, t].astype(F32))

            @pl.when(xl_n != xl)
            def _():
                for i in range(PER_PART):
                    t = part * PER_PART + i
                    x_send[t] = (y_own[xl_n, t] + y_recv[0, xl_n, t].astype(F32)
                                 + y_recv[1, xl_n, t].astype(F32) + y_recv[2, xl_n, t].astype(F32)).astype(BF16)
                send(x_send.at[tiles(part)], x_recv.at[tiles(part)], x_ss.at[part], x_rs.at[part], x_pair)

    def join_y_all(step):
        for part in range(PARTS):
            join_y(step, part)

    def before(step):
        if step == 1:
            g_wait(1, 0)
            g_wait(1, 1)
            low_stage2()
            g_send(unit(1, 0), (4, 0), x_cross)
            g_send(unit(1, 1), (4, 1), x_cross)
            g_send(own1, (5, 1), x_cross)
        if step == 2:
            g_wait(2, 0)
            low_stage3()
            g_wait(3, 0)
            g_send(unit(3, 0), (5, 0), z_next)
            g_wait(2, 1)
            g_send(unit(2, 1), (3, 1), z_prev)
            spread_pair(xs_all, in_ss, in_rs)
        if step == 3:
            g_wait(4, 0)
            g_send(unit(4, 0), (6, 0), z_prev)
            low_stage4()
            g_wait(3, 1)
        if step == 4:
            g_wait(4, 1)
            g_send(unit(4, 1), (6, 1), z_next)
            g_send(unit(2, 0), (7, 0), z_next)
            spread_pair(la, la_ss, la_rs)
        if step == 5:
            g_wait(5, 0)
            g_wait(5, 1)
            g_send(unit(5, 1), (7, 1), z_prev)
            spread_core(xs_all, in_ss, in_rs)
            spread_core(la, la_ss, la_rs)
        if step == 6:
            g_wait(6, 0)
            g_wait(6, 1)
        if step == 7:
            spread_end(la, la_ss, la_rs)
            for s in range(STEPS):
                for kind in (0, 1):
                    flip, dz = ORDER[kind][s]
                    n = ((xh + flip) % 2) * 4 + ring(z, dz)
                    la_t[pl.ds((s * 2 + kind) * ROWS, ROWS), :] = la[n * 2 + kind]
            g_wait(7, 0)
            g_wait(7, 1)

    def step_body(step, carry):
        for k in range(1, STEPS):
            @pl.when(step == k)
            def _(k=k):
                before(k)

        def tile_body(t, carry):
            rows = g[pl.ds(step * 2, 2)].reshape(2 * ROWS, F_LOCAL)
            cols = w[pl.ds(pl.multiple_of(t * TILE, TILE), TILE), :]
            acc = dot_nt(rows, cols)
            top, bottom = acc[:ROWS], acc[ROWS:]
            mine[step % 2, t] = jnp.where(c == 0, top, bottom)
            part_send[step, t] = jnp.where(c == 0, bottom, top).astype(BF16)

            @pl.when(t == 3)
            def _():
                send_part(step, 0)

            @pl.when(t == 5)
            def _():
                join_cores(step, 0)

            @pl.when(t == 6)
            def _():
                send_part(step, 1)

            @pl.when(t == 8)
            def _():
                join_cores(step, 1)

            return carry

        lax.fori_loop(0, TILES, tile_body, 0)
        send_part(step, 2)
        join_cores(step, 2)

        @pl.when(step == 5)
        def _():
            def early(s, carry):
                join_y_all(s)
                return carry

            lax.fori_loop(0, 5, early, 0)

        @pl.when(step == 6)
        def _():
            join_y_all(5)

        return carry

    lax.fori_loop(0, STEPS, step_body, 0)
    join_y_all(6)
    join_y_all(7)

    arrived(x_recv.at[tiles(0)], x_rs.at[0], x_ss.at[0])
    lg[wi] = (y_own[xl, 0] + x_recv[0].astype(F32)).astype(BF16)
    me = lg.at[wi]
    send(me, me, lg_ss.at[0], lg_rs.at[wi], partner)
    chips = [(dx, k) for dx in (0, 1) for k in (1, 3, 2, 0) if dx or k]
    for i, (dx, k) in enumerate(chips):
        send(me, me, lg_ss.at[1 + i], lg_rs.at[wi], wide_dev(xl if dx == 0 else 1 - xl, ring(y, k), c))

    scale = ADAPTER_SCALE / (16 * ROWS)

    lg_t[...] = la_t[...].T

    def gb_body(t, carry):
        cols = pl.ds(pl.multiple_of(t * TILE, TILE), TILE)
        tokens = g[:, :, cols].reshape(16 * ROWS, TILE)
        gb_ref[:, cols] = scale * dot_nn(lg_t[...], tokens)
        return carry

    lax.fori_loop(0, F_LOCAL // TILE, gb_body, 0)

    for i, (dx, k) in enumerate(chips):
        other = wide_id(xl if dx == 0 else 1 - xl, ring(y, k), c)
        blk = lg.at[other]
        arrived(blk, lg_rs.at[other], lg_ss.at[0])
        send(blk, blk, lg_ss.at[8 + i], lg_rs.at[other], partner)

    for part in range(1, PARTS):
        arrived(x_recv.at[tiles(part)], x_rs.at[part], x_ss.at[part])
    low_rows = lg[wi]

    def ig_body(t, carry):
        cols = pl.ds(pl.multiple_of(t * TILE, TILE), TILE)
        base = y_own[xl, t + 1] + x_recv[t + 1].astype(F32)
        ig_ref[:, cols] = (base + ADAPTER_SCALE * dot_nt(low_rows, a[cols, :])).astype(BF16)
        return carry

    lax.fori_loop(0, D_LOCAL // TILE, ig_body, 0)

    spread_end(xs_all, in_ss, in_rs)
    for xl_ in (0, 1):
        for y_ in range(4):
            other = wide_id(xl_, y_, 1 - c)
            arrived(lg.at[other], lg_rs.at[other], lg_ss.at[0])
    lg_t[...] = lg[...].reshape(16 * ROWS, R).T

    def ga_body(t, carry):
        cols = pl.ds(pl.multiple_of(t * TILE, TILE), TILE)
        tokens = xs_all[:, :, cols].reshape(16 * ROWS, TILE)
        ga_ref[:, cols] = scale * dot_nn(lg_t[...], tokens)
        return carry

    lax.fori_loop(0, D_LOCAL // TILE, ga_body, 0)

    for sem in g_sends:
        sent(g.at[0], g_ss.at[sem], g_rs.at[0])
    for k in range(3):
        sent(lp.at[0], l1_ss.at[k], l1_rs.at[k])
        sent(lo.at[0], l3_ss.at[k], l3_rs.at[k])
    sent(l2s, l2_ss, l2_rs)
    spread_sent(xs_all, in_ss, in_rs)
    spread_sent(la, la_ss, la_rs)
    spread_sent(lg, lg_ss, lg_rs)

    def drain(step, carry):
        xl_n, y_n = owner(step)
        for part in range(PARTS):
            sent(part_send.at[step, tiles(part)], c_ss.at[step, part], c_rs.at[step, part])

            @pl.when(y_n != y)
            def _(part=part):
                sent(part_recv.at[step, tiles(part)], y_ss.at[step, part], y_rs.at[0, 0, part])

        return carry

    lax.fori_loop(0, STEPS, drain, 0)
    for part in range(PARTS):
        sent(x_send.at[tiles(part)], x_ss.at[part], x_rs.at[part])


def shards(inputs, grad_out, w_base, adapter_down_matrix, b_factor):
    dma = pltpu.SemaphoreType.DMA
    scratch = [
        pltpu.VMEM((16, ROWS, F_LOCAL), BF16),
        pltpu.VMEM((R + D_LOCAL, F_LOCAL), BF16),
        pltpu.VMEM((D_LOCAL, R), BF16),
        pltpu.VMEM((16, ROWS, D_LOCAL), BF16),
        pltpu.VMEM((STEPS, TILES, ROWS, TILE), BF16),
        pltpu.VMEM((STEPS, TILES, ROWS, TILE), BF16),
        pltpu.VMEM((2, TILES, ROWS, TILE), F32),
        pltpu.VMEM((3, 2, TILES, ROWS, TILE), BF16),
        pltpu.VMEM((2, TILES, ROWS, TILE), F32),
        pltpu.VMEM((TILES, ROWS, TILE), BF16),
        pltpu.VMEM((TILES, ROWS, TILE), BF16),
        pltpu.VMEM((4, 56, 128), F32),
        pltpu.VMEM((3, 56, 128), F32),
        pltpu.VMEM((56, 128), F32),
        pltpu.VMEM((56, 128), F32),
        pltpu.VMEM((4, 56, 128), F32),
        pltpu.VMEM((16, ROWS, R), BF16),
        pltpu.VMEM((16 * ROWS, R), BF16),
        pltpu.VMEM((16, ROWS, R), BF16),
        pltpu.VMEM((R, 16 * ROWS), BF16),
        dma((6,)), dma((14,)), dma((16,)), dma((STEPS, PARTS)), dma((STEPS, PARTS)),
        dma((STEPS, PARTS)), dma((3, 2, PARTS)), dma((PARTS,)), dma((PARTS,)),
        dma((15,)), dma((16,)), dma((15,)), dma((16,)), dma((15,)), dma((16,)),
        dma((3,)), dma((3,)), dma(()), dma(()), dma((3,)), dma((4,)),
    ]
    any_spec = pl.BlockSpec(memory_space=pl.ANY)
    vmem_spec = pl.BlockSpec(memory_space=pltpu.VMEM)
    input_gradient, grad_a, grad_b = pl.pallas_call(
        kernel,
        out_shape=(
            jax.ShapeDtypeStruct((ROWS, D_LOCAL), BF16),
            jax.ShapeDtypeStruct((R, D_LOCAL), F32),
            jax.ShapeDtypeStruct((R, F_LOCAL), F32),
        ),
        in_specs=[any_spec] * 5,
        out_specs=(vmem_spec,) * 3,
        scratch_shapes=scratch,
        compiler_params=pltpu.CompilerParams(
            collective_id=0, has_side_effects=True, vmem_limit_bytes=67043328
        ),
        name="backward",
    )(inputs, grad_out, w_base, adapter_down_matrix, b_factor)
    return input_gradient, grad_a.T, grad_b


def solution(mesh):
    return jax.shard_map(
        shards,
        mesh=mesh,
        in_specs=(
            P("wide", "narrow"),
            P("narrow", "wide"),
            P("narrow", "wide"),
            P("narrow", None),
            P(None, "wide"),
        ),
        out_specs=(P("wide", "narrow"), P("narrow", None), P(None, "wide")),
        check_vma=False,
    )
```

time: 535 us -> 170 us (0.32)
  waiting for transfers between devices: 397 us -> 0 us
  Pallas kernels: 0 us -> 162 us
  blocking collectives: 62.6 us -> 0 us
  matrix products: 47.7 us -> 0 us
  between operations: 13.8 us -> 0.65 us
  other arithmetic: 5.99 us -> 0 us
    pallas_call x0 -> x1, Pallas kernels: none -> 162 us  [shards(): pl.pallas_call(kernel, out_shape=(jax.ShapeDtypeStruct((ROWS, D_LOCAL), B...]
    psum x2 -> x0, waiting for transfers between devices: 159 us -> none  [the longest x1 102 us: shards(): lax.psum(adapter_matrix * contract_first(low_mine, grad_out), 'narrow')]
    all_gather x1 -> x0, waiting for transfers between devices: 142 us -> none  [shards(): block_rows = lax.all_gather(grad_out, 'narrow', axis=0, tiled=True)]
    reduce_scatter x1 -> x0, waiting for transfers between devices: 94.8 us -> none  [shards(): summed = lax.psum_scatter(stacked, 'wide', scatter_dimension=0, tiled=True)]
    dot_general x6 -> x0, matrix products: 47.7 us -> none  [the longest x3 42.3 us: contract_trailing_axis(): lax.dot_general(left, right, (((1,), (1,)), ((), ())), preferred_element_...]
    psum x1 -> x0, blocking collectives: 43 us -> none  [shards(): low_act = lax.psum(low_part, 'narrow').astype(jnp.bfloat16)]
    all_gather x1 -> x0, blocking collectives: 19.6 us -> none  [shards(): low_all = lax.all_gather(low_act, 'wide', axis=0, tiled=True)]
    concatenate x1 -> x0, other arithmetic: 5.99 us -> none  [shards(): stacked = jnp.concatenate([base_part, low_part], axis=1)]
  transfers between devices with their start and end apart: 4 -> 0, of which waited for: 4 -> 0; matrix products, arithmetic and copies ran while one was open for 2% -> 0% of each run, Pallas kernels for 0% -> 0%
where the time goes in v1:
time: 170 us
  Pallas kernels  162 us (95%)
  local copies, waits for them, and re-layouts  6.61 us (4%)
    pallas_call x1, Pallas kernels, shards(): pl.pallas_call(kernel, out_shape=(jax.ShapeDtypeStruct((ROWS, D_LOCAL), B...  162 us
    unnamed x5, local copies, waits for them, and re-layouts  6.61 us

profile of v1, /device:TPU:2, one launch (start us, length us, event | category | flops | bytes accessed | tf_op | source)
XLA Modules:
  0.0 169.6 jit_solution(13274662212755977929)
XLA Ops:
  0.6 162.4 %backward.1 = (bf16[112,2048]{1,0:T(8,128)(2,1)}, f32[256,2048]{1,0:T(8,128)}, f32[256,3328]{1,0:T(8,128)}) custom-call(bf16[112,2048]{1,0:T(8,128)(2,1)} %x_hbm.1, bf16[224,3328]{1,0:T(8,128)(2,1)} %g_hbm.1, bf16[2048,3328]{1,0:T(8,128)(2,1)} %w_hbm.1, bf16[2048,256]{1,0:T(8,128)(2,1)} %a_hbm.1, bf16[256,3328]{1,0:T(8,128)(2,1)} %b_hbm.1), custom_call_target="tpu_custom_call" | custom-call | tf_op jit(solution)/shard_map/backward/pallas_call | solution.py:477
  163.0 0.0 copy-start
  163.0 3.0 %copy.8 = f32[2048,256]{1,0:T(8,128)} copy(f32[2048,256]{0,1:T(8,128)} %bitcast.1) | data formatting | bytes 4194304
  166.1 1.8 %copy.11 = bf16[112,2048]{1,0:T(8,128)(2,1)} copy(bf16[112,2048]{1,0:T(8,128)(2,1)} %get-tuple-element.15) | data formatting | bytes 917504
  167.9 0.0 copy-done
  167.9 1.8 %copy.12 = f32[256,3328]{1,0:T(8,128)} copy(f32[256,3328]{1,0:T(8,128)S(1)} %copy-done) | data formatting | bytes 6815744
Async XLA Ops:
  163.0 4.9 %copy-start = (f32[256,3328]{1,0:T(8,128)S(1)}, f32[256,3328]{1,0:T(8,128)}, u32[]{:S(2)}) copy-start(f32[256,3328]{1,0:T(8,128)} %get-tuple-element.17) | copy-start | bytes 10223620

commit v2 on v1

--- a/solution.py
+++ b/solution.py
@@ -14,14 +14,17 @@
 TILES = (R + D_LOCAL) // TILE
 PARTS = 3
 PER_PART = TILES // PARTS
+HALF = TILE // 2
+PASSED = (0, 0, 0, 1, 2, 2, 5, 6, 7)
+CUTS = ((0, 64), (64, 48))
 STEPS = 8
 MESH = pl.DeviceIdType.MESH
 BF16 = jnp.bfloat16
 F32 = jnp.float32
 
 ORDER = (
-    ((0, 0), (0, 1), (1, 0), (0, 3), (1, 1), (0, 2), (1, 2), (1, 3)),
-    ((0, 0), (0, 3), (0, 1), (0, 2), (1, 3), (1, 0), (1, 2), (1, 1)),
+    ((0, 0), (0, 1), (1, 0), (0, 3), (1, 3), (1, 1), (0, 2), (1, 2)),
+    ((0, 0), (0, 3), (0, 1), (1, 0), (0, 2), (1, 1), (1, 3), (1, 2)),
 )
 
 
@@ -37,7 +40,7 @@
     if isinstance(index, int):
         return values[index]
     out = index * 0 + values[0]
-    for i, value in enumerate(values[1:], 1):
+    for i, value in enumerate(values[1:STEPS], 1):
         out = out + (index == i).astype(jnp.int32) * (value - values[0])
     return out
 
@@ -45,9 +48,9 @@
 def kernel(
     x_hbm, g_hbm, w_hbm, a_hbm, b_hbm,
     ig_ref, ga_ref, gb_ref,
-    g, w, a, xs_all, part_send, part_recv, mine, y_recv, y_own, x_send, x_recv,
+    g, w, a, xs_all, part_send, part_recv, mine, relay, y_recv, y_own, x_send, x_recv,
     lp, l1, l2s, l2r, lo, la, la_t, lg, lg_t,
-    ld_sem, g_ss, g_rs, c_ss, c_rs, y_ss, y_rs, x_ss, x_rs,
+    ld_sem, g_ss, g_rs, c_ss, c_rs, f_rs, y_ss, y_rs, x_ss, x_rs,
     in_ss, in_rs, la_ss, la_rs, lg_ss, lg_rs, l1_ss, l1_rs, l2_ss, l2_rs, l3_ss, l3_rs,
 ):
     wi = lax.axis_index("wide")
@@ -110,18 +113,24 @@
 
     g_sends = []
 
-    def g_send(src, dst, dev):
-        slot = dst[0] * 2 + dst[1]
-        sem = len(g_sends)
-        send(src, g.at[slot], g_ss.at[sem], g_rs.at[slot], dev)
-        g_sends.append(sem)
-
-    def g_wait(step, kind):
-        slot = step * 2 + kind
-        arrived(g.at[slot], g_rs.at[slot], g_ss.at[0])
-
-    def unit(step, kind):
-        return g.at[step * 2 + kind]
+    def g_slot(unit, cut):
+        slot = unit[0] * 2 + unit[1]
+        if cut is None:
+            return g.at[slot], slot
+        return g.at[slot, pl.ds(*CUTS[cut])], slot if cut == 0 else 16 + unit[0] - 6
+
+    def g_send(src, dst, dev, cut=None):
+        ref, sem = g_slot(dst, cut)
+        if isinstance(src, tuple):
+            src = g_slot(src, cut)[0]
+        elif cut is not None:
+            src = src.at[pl.ds(*CUTS[cut])]
+        send(src, ref, g_ss.at[len(g_sends)], g_rs.at[sem], dev)
+        g_sends.append(cut)
+
+    def g_wait(step, kind, cut=None):
+        ref, sem = g_slot((step, kind), cut)
+        arrived(ref, g_rs.at[sem], g_ss.at[0])
 
     own0, own1 = g_hbm.at[pl.ds(0, ROWS)], g_hbm.at[pl.ds(ROWS, ROWS)]
     g_send(own0, (2, 0), x_cross)
@@ -199,6 +208,7 @@
         spread_own(la, la_ss, la_rs)
 
     low_stage1()
+    g_send(own1, (3, 1), x_cross)
     g_send(own0, (3, 0), z_next)
     g_send(own1, (2, 1), z_prev)
 
@@ -212,104 +222,140 @@
         )
         return (xh + flip) % 2, ring(z, dz)
 
-    def tiles(part):
-        return pl.ds(part * PER_PART, PER_PART)
-
     def send_part(step, part):
-        send(part_send.at[step, tiles(part)], part_recv.at[step, tiles(part)],
+        send(part_send.at[step, part], part_recv.at[step, part],
              c_ss.at[step, part], c_rs.at[step, part], partner)
 
     def join_cores(step, part):
         xl_n, y_n = owner(step)
-        ref = part_recv.at[step, tiles(part)]
-        arrived(ref, c_rs.at[step, part], c_ss.at[step, part])
+        d = (y - y_n + 4) % 4
+        arrived(part_recv.at[step, part], c_rs.at[step, part], c_ss.at[step, part])
+
+        def total(h, i):
+            return mine[step % 4, part, h, i] + part_recv[step, part, h, i].astype(F32)
+
+        @pl.when(d == 0)
+        def _():
+            for h in (0, 1):
+                for i in range(PER_PART):
+                    y_own[xl_n, part, h, i] = total(h, i)
+
+        @pl.when(d == 2)
+        def _():
+            for h in (0, 1):
+                for i in range(PER_PART):
+                    part_recv[step, part, h, i] = total(h, i).astype(BF16)
+            for h, k in ((0, 3), (1, 1)):
+                send(part_recv.at[step, part, h], relay.at[h, xl_n, part], y_ss.at[step, part, h],
+                     f_rs.at[h, xl_n, part], wide_dev(xl, ring(y, k), c))
+
+        @pl.when(d % 2 == 1)
+        def _():
+            late = d // 2
+            for i in range(PER_PART):
+                mine[step % 4, part, late, i] = total(late, i)
+                part_recv[step, part, 1 - late, i] = total(1 - late, i).astype(BF16)
+            send(part_recv.at[step, part, 1 - late], y_recv.at[late, xl_n, part, 1 - late],
+                 y_ss.at[step, part, 1 - late], y_rs.at[late, xl_n, part, 1 - late], wide_dev(xl, y_n, c))
+
+    def pass_on(step, part):
+        xl_n, y_n = owner(step)
+        d = (y - y_n + 4) % 4
+
+        @pl.when(d % 2 == 1)
+        def _():
+            late = d // 2
+            arrived(relay.at[late, xl_n, part], f_rs.at[late, xl_n, part], x_ss.at[part])
+            for i in range(PER_PART):
+                part_recv[step, part, late, i] = (
+                    mine[step % 4, part, late, i] + relay[late, xl_n, part, i].astype(F32)
+                ).astype(BF16)
+            send(part_recv.at[step, part, late], y_recv.at[late, xl_n, part, late],
+                 y_ss.at[step, part, late], y_rs.at[late, xl_n, part, late], wide_dev(xl, y_n, c))
+
+    def join_y(step, part):
+        xl_n, y_n = owner(step)
 
         @pl.when(y_n == y)
         def _():
-            for i in range(PER_PART):
-                t = part * PER_PART + i
-                y_own[xl_n, t] = mine[step % 2, t] + part_recv[step, t].astype(F32)
-
-        @pl.when(y_n != y)
-        def _():
-            for i in range(PER_PART):
-                t = part * PER_PART + i
-                part_recv[step, t] = (mine[step % 2, t] + part_recv[step, t].astype(F32)).astype(BF16)
-            r = (y - y_n + 4) % 4 - 1
-            send(ref, y_recv.at[r, xl_n, tiles(part)], y_ss.at[step, part], y_rs.at[r, xl_n, part],
-                 wide_dev(xl, y_n, c))
-
-    def join_y(step, part):
-        xl_n, y_n = owner(step)
-
-        @pl.when(y_n == y)
-        def _():
-            for r in range(3):
-                arrived(y_recv.at[r, xl_n, tiles(part)], y_rs.at[r, xl_n, part], x_ss.at[part])
+            for r in (0, 1):
+                for h in (0, 1):
+                    arrived(y_recv.at[r, xl_n, part, h], y_rs.at[r, xl_n, part, h], x_ss.at[part])
+
+            def total(h, i):
+                return (y_own[xl_n, part, h, i] + y_recv[0, xl_n, part, h, i].astype(F32)
+                        + y_recv[1, xl_n, part, h, i].astype(F32))
 
             @pl.when(xl_n == xl)
             def _():
-                for i in range(PER_PART):
-                    t = part * PER_PART + i
-                    y_own[xl_n, t] += (y_recv[0, xl_n, t].astype(F32) + y_recv[1, xl_n, t].astype(F32)
-                                       + y_recv[2, xl_n, t].astype(F32))
+                for h in (0, 1):
+                    for i in range(PER_PART):
+                        y_own[xl_n, part, h, i] = total(h, i)
 
             @pl.when(xl_n != xl)
             def _():
-                for i in range(PER_PART):
-                    t = part * PER_PART + i
-                    x_send[t] = (y_own[xl_n, t] + y_recv[0, xl_n, t].astype(F32)
-                                 + y_recv[1, xl_n, t].astype(F32) + y_recv[2, xl_n, t].astype(F32)).astype(BF16)
-                send(x_send.at[tiles(part)], x_recv.at[tiles(part)], x_ss.at[part], x_rs.at[part], x_pair)
+                for h in (0, 1):
+                    for i in range(PER_PART):
+                        x_send[part, h, i] = total(h, i).astype(BF16)
+                send(x_send.at[part], x_recv.at[part], x_ss.at[part], x_rs.at[part], x_pair)
+
+    def over_parts(do, step):
+        def body(part, carry):
+            do(step, part)
+            return carry
+
+        return lax.fori_loop(0, PARTS, body, 0)
+
+    def pass_on_all(step):
+        return over_parts(pass_on, step)
 
     def join_y_all(step):
-        for part in range(PARTS):
-            join_y(step, part)
+        return over_parts(join_y, step)
+
+    def own_total(part, h, i):
+        return y_own[xl, part, h, i] + x_recv[part, h, i].astype(F32)
 
     def before(step):
         if step == 1:
             g_wait(1, 0)
+            low_stage2()
+            g_send((1, 0), (5, 0), x_cross)
             g_wait(1, 1)
-            low_stage2()
-            g_send(unit(1, 0), (4, 0), x_cross)
-            g_send(unit(1, 1), (4, 1), x_cross)
-            g_send(own1, (5, 1), x_cross)
+            g_send(g.at[3], (6, 1), x_cross, 0)
+            g_send(g.at[3], (6, 1), x_cross, 1)
         if step == 2:
             g_wait(2, 0)
-            low_stage3()
+            g_send((2, 0), (4, 0), z_next)
+            g_wait(2, 1)
+            g_send((2, 1), (4, 1), z_prev)
             g_wait(3, 0)
-            g_send(unit(3, 0), (5, 0), z_next)
-            g_wait(2, 1)
-            g_send(unit(2, 1), (3, 1), z_prev)
+            g_send((3, 0), (6, 0), z_next)
             spread_pair(xs_all, in_ss, in_rs)
         if step == 3:
+            g_wait(3, 1)
+            g_send((3, 1), (5, 1), z_prev)
+            low_stage3()
+        if step == 4:
             g_wait(4, 0)
-            g_send(unit(4, 0), (6, 0), z_prev)
-            low_stage4()
-            g_wait(3, 1)
-        if step == 4:
             g_wait(4, 1)
-            g_send(unit(4, 1), (6, 1), z_next)
-            g_send(unit(2, 0), (7, 0), z_next)
-            spread_pair(la, la_ss, la_rs)
         if step == 5:
             g_wait(5, 0)
+            g_send((5, 0), (7, 0), z_prev)
+            spread_core(xs_all, in_ss, in_rs)
+            g_wait(6, 1, 0)
+            g_send((6, 1), (7, 1), z_next, 0)
             g_wait(5, 1)
-            g_send(unit(5, 1), (7, 1), z_prev)
-            spread_core(xs_all, in_ss, in_rs)
-            spread_core(la, la_ss, la_rs)
+            low_stage4()
         if step == 6:
             g_wait(6, 0)
-            g_wait(6, 1)
+            g_wait(6, 1, 1)
+            g_send((6, 1), (7, 1), z_next, 1)
+            spread_pair(la, la_ss, la_rs)
         if step == 7:
-            spread_end(la, la_ss, la_rs)
-            for s in range(STEPS):
-                for kind in (0, 1):
-                    flip, dz = ORDER[kind][s]
-                    n = ((xh + flip) % 2) * 4 + ring(z, dz)
-                    la_t[pl.ds((s * 2 + kind) * ROWS, ROWS), :] = la[n * 2 + kind]
+            spread_core(la, la_ss, la_rs)
             g_wait(7, 0)
-            g_wait(7, 1)
+            g_wait(7, 1, 0)
+            g_wait(7, 1, 1)
 
     def step_body(step, carry):
         for k in range(1, STEPS):
@@ -322,24 +368,31 @@
             cols = w[pl.ds(pl.multiple_of(t * TILE, TILE), TILE), :]
             acc = dot_nt(rows, cols)
             top, bottom = acc[:ROWS], acc[ROWS:]
-            mine[step % 2, t] = jnp.where(c == 0, top, bottom)
-            part_send[step, t] = jnp.where(c == 0, bottom, top).astype(BF16)
+            keep, give = jnp.where(c == 0, top, bottom), jnp.where(c == 0, bottom, top).astype(BF16)
+            part, i = t // PER_PART, t % PER_PART
+            for h in (0, 1):
+                mine[step % 4, part, h, i] = keep[:, h * HALF:h * HALF + HALF]
+                part_send[step, part, h, i] = give[:, h * HALF:h * HALF + HALF]
+
+            @pl.when(t == 4)
+            def _():
+                lax.fori_loop(pick(step, PASSED), pick(step, PASSED[1:]), lambda s, carry: pass_on_all(s), 0)
+
+            @pl.when(((t == 8) & (step == 6)) | ((t == 4) & (step == 7)))
+            def _():
+                join_y_all(step - 2)
 
             @pl.when(t == 3)
             def _():
                 send_part(step, 0)
 
-            @pl.when(t == 5)
-            def _():
-                join_cores(step, 0)
+            @pl.when((t == 5) | (t == 8))
+            def _():
+                join_cores(step, t // 4 - 1)
 
             @pl.when(t == 6)
             def _():
                 send_part(step, 1)
-
-            @pl.when(t == 8)
-            def _():
-                join_cores(step, 1)
 
             return carry
 
@@ -353,20 +406,17 @@
                 join_y_all(s)
                 return carry
 
-            lax.fori_loop(0, 5, early, 0)
-
-        @pl.when(step == 6)
-        def _():
-            join_y_all(5)
+            lax.fori_loop(0, 4, early, 0)
 
         return carry
 
     lax.fori_loop(0, STEPS, step_body, 0)
+    pass_on_all(7)
     join_y_all(6)
     join_y_all(7)
 
-    arrived(x_recv.at[tiles(0)], x_rs.at[0], x_ss.at[0])
-    lg[wi] = (y_own[xl, 0] + x_recv[0].astype(F32)).astype(BF16)
+    arrived(x_recv.at[0], x_rs.at[0], x_ss.at[0])
+    lg[wi] = jnp.concatenate([own_total(0, 0, 0), own_total(0, 1, 0)], axis=1).astype(BF16)
     me = lg.at[wi]
     send(me, me, lg_ss.at[0], lg_rs.at[wi], partner)
     chips = [(dx, k) for dx in (0, 1) for k in (1, 3, 2, 0) if dx or k]
@@ -375,6 +425,12 @@
 
     scale = ADAPTER_SCALE / (16 * ROWS)
 
+    spread_end(la, la_ss, la_rs)
+    for s in range(STEPS):
+        for kind in (0, 1):
+            flip, dz = ORDER[kind][s]
+            n = ((xh + flip) % 2) * 4 + ring(z, dz)
+            la_t[pl.ds((s * 2 + kind) * ROWS, ROWS), :] = la[n * 2 + kind]
     lg_t[...] = la_t[...].T
 
     def gb_body(t, carry):
@@ -392,12 +448,13 @@
         send(blk, blk, lg_ss.at[8 + i], lg_rs.at[other], partner)
 
     for part in range(1, PARTS):
-        arrived(x_recv.at[tiles(part)], x_rs.at[part], x_ss.at[part])
+        arrived(x_recv.at[part], x_rs.at[part], x_ss.at[part])
     low_rows = lg[wi]
 
     def ig_body(t, carry):
         cols = pl.ds(pl.multiple_of(t * TILE, TILE), TILE)
-        base = y_own[xl, t + 1] + x_recv[t + 1].astype(F32)
+        part, i = (t + 1) // PER_PART, (t + 1) % PER_PART
+        base = jnp.concatenate([own_total(part, 0, i), own_total(part, 1, i)], axis=1)
         ig_ref[:, cols] = (base + ADAPTER_SCALE * dot_nt(low_rows, a[cols, :])).astype(BF16)
         return carry
 
@@ -418,8 +475,8 @@
 
     lax.fori_loop(0, D_LOCAL // TILE, ga_body, 0)
 
-    for sem in g_sends:
-        sent(g.at[0], g_ss.at[sem], g_rs.at[0])
+    for sem, cut in enumerate(g_sends):
+        sent(g_slot((0, 0), None)[0] if cut is None else g.at[0, pl.ds(*CUTS[cut])], g_ss.at[sem], g_rs.at[0])
     for k in range(3):
         sent(lp.at[0], l1_ss.at[k], l1_rs.at[k])
         sent(lo.at[0], l3_ss.at[k], l3_rs.at[k])
@@ -431,33 +488,36 @@
     def drain(step, carry):
         xl_n, y_n = owner(step)
         for part in range(PARTS):
-            sent(part_send.at[step, tiles(part)], c_ss.at[step, part], c_rs.at[step, part])
+            sent(part_send.at[step, part], c_ss.at[step, part], c_rs.at[step, part])
 
             @pl.when(y_n != y)
             def _(part=part):
-                sent(part_recv.at[step, tiles(part)], y_ss.at[step, part], y_rs.at[0, 0, part])
+                for h in (0, 1):
+                    sent(part_recv.at[step, part, h], y_ss.at[step, part, h], y_rs.at[0, 0, part, h])
 
         return carry
 
     lax.fori_loop(0, STEPS, drain, 0)
     for part in range(PARTS):
-        sent(x_send.at[tiles(part)], x_ss.at[part], x_rs.at[part])
+        sent(x_send.at[part], x_ss.at[part], x_rs.at[part])
 
 
 def shards(inputs, grad_out, w_base, adapter_down_matrix, b_factor):
     dma = pltpu.SemaphoreType.DMA
+    pieces = (PARTS, 2, PER_PART, ROWS, HALF)
     scratch = [
         pltpu.VMEM((16, ROWS, F_LOCAL), BF16),
         pltpu.VMEM((R + D_LOCAL, F_LOCAL), BF16),
         pltpu.VMEM((D_LOCAL, R), BF16),
         pltpu.VMEM((16, ROWS, D_LOCAL), BF16),
-        pltpu.VMEM((STEPS, TILES, ROWS, TILE), BF16),
-        pltpu.VMEM((STEPS, TILES, ROWS, TILE), BF16),
-        pltpu.VMEM((2, TILES, ROWS, TILE), F32),
-        pltpu.VMEM((3, 2, TILES, ROWS, TILE), BF16),
-        pltpu.VMEM((2, TILES, ROWS, TILE), F32),
-        pltpu.VMEM((TILES, ROWS, TILE), BF16),
-        pltpu.VMEM((TILES, ROWS, TILE), BF16),
+        pltpu.VMEM((STEPS,) + pieces, BF16),
+        pltpu.VMEM((STEPS,) + pieces, BF16),
+        pltpu.VMEM((4,) + pieces, F32),
+        pltpu.VMEM((2, 2, PARTS, PER_PART, ROWS, HALF), BF16),
+        pltpu.VMEM((2, 2) + pieces, BF16),
+        pltpu.VMEM((2,) + pieces, F32),
+        pltpu.VMEM(pieces, BF16),
+        pltpu.VMEM(pieces, BF16),
         pltpu.VMEM((4, 56, 128), F32),
         pltpu.VMEM((3, 56, 128), F32),
         pltpu.VMEM((56, 128), F32),
@@ -467,8 +527,8 @@
         pltpu.VMEM((16 * ROWS, R), BF16),
         pltpu.VMEM((16, ROWS, R), BF16),
         pltpu.VMEM((R, 16 * ROWS), BF16),
-        dma((6,)), dma((14,)), dma((16,)), dma((STEPS, PARTS)), dma((STEPS, PARTS)),
-        dma((STEPS, PARTS)), dma((3, 2, PARTS)), dma((PARTS,)), dma((PARTS,)),
+        dma((6,)), dma((16,)), dma((18,)), dma((STEPS, PARTS)), dma((STEPS, PARTS)),
+        dma((2, 2, PARTS)), dma((STEPS, PARTS, 2)), dma((2, 2, PARTS, 2)), dma((PARTS,)), dma((PARTS,)),
         dma((15,)), dma((16,)), dma((15,)), dma((16,)), dma((15,)), dma((16,)),
         dma((3,)), dma((3,)), dma(()), dma(()), dma((3,)), dma((4,)),
     ]

time: 170 us -> 152 us (0.89)
  Pallas kernels: 162 us -> 144 us
    pallas_call x1, Pallas kernels: 162 us -> 144 us  [shards(): pl.pallas_call(kernel, out_shape=(jax.ShapeDtypeStruct((ROWS, D_LOCAL), B...]
where the time goes in v2:
time: 152 us; the launch traced here: 151 us
  Pallas kernels  144 us (95%)
  local copies, waits for them, and re-layouts  6.61 us (4%)
    pallas_call x1, Pallas kernels, shards(): pl.pallas_call(kernel, out_shape=(jax.ShapeDtypeStruct((ROWS, D_LOCAL), B...  144 us
    unnamed x5, local copies, waits for them, and re-layouts  6.61 us

profile of v2, /device:TPU:2, one launch (start us, length us, event | category | flops | bytes accessed | tf_op | source)
XLA Modules:
  0.0 151.2 jit_solution(4061159239767144436)
XLA Ops:
  0.6 143.9 %backward.1 = (bf16[112,2048]{1,0:T(8,128)(2,1)}, f32[256,2048]{1,0:T(8,128)}, f32[256,3328]{1,0:T(8,128)}) custom-call(bf16[112,2048]{1,0:T(8,128)(2,1)} %x_hbm.1, bf16[224,3328]{1,0:T(8,128)(2,1)} %g_hbm.1, bf16[2048,3328]{1,0:T(8,128)(2,1)} %w_hbm.1, bf16[2048,256]{1,0:T(8,128)(2,1)} %a_hbm.1, bf16[256,3328]{1,0:T(8,128)(2,1)} %b_hbm.1), custom_call_target="tpu_custom_call" | custom-call | tf_op jit(solution)/shard_map/backward/pallas_call | solution.py:537
  144.6 0.0 copy-start
  144.6 3.0 %copy.8 = f32[2048,256]{1,0:T(8,128)} copy(f32[2048,256]{0,1:T(8,128)} %bitcast.1) | data formatting | bytes 4194304
  147.6 1.8 %copy.11 = bf16[112,2048]{1,0:T(8,128)(2,1)} copy(bf16[112,2048]{1,0:T(8,128)(2,1)} %get-tuple-element.15) | data formatting | bytes 917504
  149.4 0.0 copy-done
  149.4 1.8 %copy.12 = f32[256,3328]{1,0:T(8,128)} copy(f32[256,3328]{1,0:T(8,128)S(1)} %copy-done) | data formatting | bytes 6815744
Async XLA Ops:
  144.6 4.9 %copy-start = (f32[256,3328]{1,0:T(8,128)S(1)}, f32[256,3328]{1,0:T(8,128)}, u32[]{:S(2)}) copy-start(f32[256,3328]{1,0:T(8,128)} %get-tuple-element.17) | copy-start | bytes 10223620

commit v3 on v2

--- a/solution.py
+++ b/solution.py
@@ -16,6 +16,8 @@
 PER_PART = TILES // PARTS
 HALF = TILE // 2
 PASSED = (0, 0, 0, 1, 2, 2, 5, 6, 7)
+JOINED = (0, 0, 0, 0, 0, 0, 2, 4, 6)
+CHIPS = ((0, 1), (0, 3), (0, 2), (1, 0), (1, 1), (1, 3), (1, 2))
 CUTS = ((0, 64), (64, 48))
 STEPS = 8
 MESH = pl.DeviceIdType.MESH
@@ -23,7 +25,7 @@
 F32 = jnp.float32
 
 ORDER = (
-    ((0, 0), (0, 1), (1, 0), (0, 3), (1, 3), (1, 1), (0, 2), (1, 2)),
+    ((0, 0), (0, 1), (1, 0), (0, 3), (1, 3), (0, 2), (1, 1), (1, 2)),
     ((0, 0), (0, 3), (0, 1), (1, 0), (0, 2), (1, 1), (1, 3), (1, 2)),
 )
 
@@ -144,23 +146,22 @@
             send(me, me, ss.at[k], rs.at[wi], wide_dev(xl, ring(y, k), c))
         send(me, me, ss.at[4], rs.at[wi], partner)
 
-    def spread_pair(buf, ss, rs):
+    def spread_pair(buf, ss, rs, near=True, far=True):
         other = wide_id(1 - xl, y, c)
         blk = buf.at[other]
-        arrived(blk, rs.at[other], ss.at[0])
+        if near:
+            arrived(blk, rs.at[other], ss.at[0])
+            send(blk, blk, ss.at[8], rs.at[other], partner)
         for i, k in enumerate((1, 3, 2)):
-            send(blk, blk, ss.at[5 + i], rs.at[other], wide_dev(xl, ring(y, k), c))
-        send(blk, blk, ss.at[8], rs.at[other], partner)
-
-    def spread_core(buf, ss, rs):
-        i = 9
-        for xl_ in (xl, 1 - xl):
-            for k in (1, 3, 2):
-                other = wide_id(xl_, ring(y, k), c)
-                blk = buf.at[other]
-                arrived(blk, rs.at[other], ss.at[0])
-                send(blk, blk, ss.at[i], rs.at[other], partner)
-                i += 1
+            if near and k != 2 or far and k == 2:
+                send(blk, blk, ss.at[5 + i], rs.at[other], wide_dev(xl, ring(y, k), c))
+
+    def spread_core(buf, ss, rs, blocks=range(6)):
+        for i in blocks:
+            other = wide_id(xl if i < 3 else 1 - xl, ring(y, (1, 3, 2)[i % 3]), c)
+            blk = buf.at[other]
+            arrived(blk, rs.at[other], ss.at[0])
+            send(blk, blk, ss.at[9 + i], rs.at[other], partner)
 
     def spread_end(buf, ss, rs):
         for xl_ in (0, 1):
@@ -208,7 +209,6 @@
         spread_own(la, la_ss, la_rs)
 
     low_stage1()
-    g_send(own1, (3, 1), x_cross)
     g_send(own0, (3, 0), z_next)
     g_send(own1, (2, 1), z_prev)
 
@@ -315,39 +315,58 @@
     def own_total(part, h, i):
         return y_own[xl, part, h, i] + x_recv[part, h, i].astype(F32)
 
+    def announce_all(step):
+        xl_n, y_n = owner(step)
+
+        @pl.when((xl_n == xl) & (y_n == y))
+        def _():
+            arrived(x_recv.at[0], x_rs.at[0], x_ss.at[0])
+            lg[wi] = jnp.concatenate([own_total(0, 0, 0), own_total(0, 1, 0)], axis=1).astype(BF16)
+            me = lg.at[wi]
+            send(me, me, lg_ss.at[0], lg_rs.at[wi], partner)
+            for i, (dx, k) in enumerate(CHIPS):
+                send(me, me, lg_ss.at[1 + i], lg_rs.at[wi], wide_dev((xl + dx) % 2, ring(y, k), c))
+
+        return 0
+
     def before(step):
         if step == 1:
             g_wait(1, 0)
             low_stage2()
-            g_send((1, 0), (5, 0), x_cross)
+            g_send(g_hbm.at[pl.ds(ROWS, ROWS)], (3, 1), x_cross)
+            g_send((1, 0), (6, 0), x_cross)
             g_wait(1, 1)
             g_send(g.at[3], (6, 1), x_cross, 0)
             g_send(g.at[3], (6, 1), x_cross, 1)
         if step == 2:
             g_wait(2, 0)
             g_send((2, 0), (4, 0), z_next)
+            low_stage3()
             g_wait(2, 1)
             g_send((2, 1), (4, 1), z_prev)
             g_wait(3, 0)
-            g_send((3, 0), (6, 0), z_next)
-            spread_pair(xs_all, in_ss, in_rs)
+            g_send((3, 0), (5, 0), z_next)
+            spread_pair(xs_all, in_ss, in_rs, far=False)
         if step == 3:
             g_wait(3, 1)
             g_send((3, 1), (5, 1), z_prev)
-            low_stage3()
+            spread_pair(xs_all, in_ss, in_rs, near=False)
         if step == 4:
+            g_wait(4, 1)
             g_wait(4, 0)
-            g_wait(4, 1)
+            low_stage4()
         if step == 5:
-            g_wait(5, 0)
-            g_send((5, 0), (7, 0), z_prev)
-            spread_core(xs_all, in_ss, in_rs)
+            g_wait(6, 0)
+            g_send((6, 0), (7, 0), z_prev)
+            spread_core(xs_all, in_ss, in_rs, range(3))
+            join_y_all(0)
+            join_y_all(1)
             g_wait(6, 1, 0)
             g_send((6, 1), (7, 1), z_next, 0)
+            g_wait(5, 0)
             g_wait(5, 1)
-            low_stage4()
         if step == 6:
-            g_wait(6, 0)
+            spread_core(xs_all, in_ss, in_rs, range(3, 6))
             g_wait(6, 1, 1)
             g_send((6, 1), (7, 1), z_next, 1)
             spread_pair(la, la_ss, la_rs)
@@ -374,13 +393,13 @@
                 mine[step % 4, part, h, i] = keep[:, h * HALF:h * HALF + HALF]
                 part_send[step, part, h, i] = give[:, h * HALF:h * HALF + HALF]
 
-            @pl.when(t == 4)
+            @pl.when(t == 4 + 3 * (step >= 6).astype(jnp.int32))
             def _():
                 lax.fori_loop(pick(step, PASSED), pick(step, PASSED[1:]), lambda s, carry: pass_on_all(s), 0)
 
-            @pl.when(((t == 8) & (step == 6)) | ((t == 4) & (step == 7)))
-            def _():
-                join_y_all(step - 2)
+            @pl.when((t == 8) & (step >= 6))
+            def _():
+                lax.fori_loop(pick(step, JOINED), pick(step, JOINED[1:]), lambda s, carry: join_y_all(s), 0)
 
             @pl.when(t == 3)
             def _():
@@ -400,28 +419,12 @@
         send_part(step, 2)
         join_cores(step, 2)
 
-        @pl.when(step == 5)
-        def _():
-            def early(s, carry):
-                join_y_all(s)
-                return carry
-
-            lax.fori_loop(0, 4, early, 0)
-
         return carry
 
     lax.fori_loop(0, STEPS, step_body, 0)
     pass_on_all(7)
     join_y_all(6)
-    join_y_all(7)
-
-    arrived(x_recv.at[0], x_rs.at[0], x_ss.at[0])
-    lg[wi] = jnp.concatenate([own_total(0, 0, 0), own_total(0, 1, 0)], axis=1).astype(BF16)
-    me = lg.at[wi]
-    send(me, me, lg_ss.at[0], lg_rs.at[wi], partner)
-    chips = [(dx, k) for dx in (0, 1) for k in (1, 3, 2, 0) if dx or k]
-    for i, (dx, k) in enumerate(chips):
-        send(me, me, lg_ss.at[1 + i], lg_rs.at[wi], wide_dev(xl if dx == 0 else 1 - xl, ring(y, k), c))
+    lax.fori_loop(0, 6, lambda s, carry: announce_all(s), 0)
 
     scale = ADAPTER_SCALE / (16 * ROWS)
 
@@ -441,14 +444,27 @@
 
     lax.fori_loop(0, F_LOCAL // TILE, gb_body, 0)
 
-    for i, (dx, k) in enumerate(chips):
-        other = wide_id(xl if dx == 0 else 1 - xl, ring(y, k), c)
+    announce_all(6)
+    join_y_all(7)
+    announce_all(7)
+    for i, (dx, k) in enumerate(CHIPS):
+        other = wide_id((xl + dx) % 2, ring(y, k), c)
         blk = lg.at[other]
         arrived(blk, lg_rs.at[other], lg_ss.at[0])
         send(blk, blk, lg_ss.at[8 + i], lg_rs.at[other], partner)
 
-    for part in range(1, PARTS):
-        arrived(x_recv.at[part], x_rs.at[part], x_ss.at[part])
+    spread_end(xs_all, in_ss, in_rs)
+    spread_end(lg, lg_ss, lg_rs)
+    lg_t[...] = lg[...].reshape(16 * ROWS, R).T
+
+    def ga_body(t, carry):
+        cols = pl.ds(pl.multiple_of(t * TILE, TILE), TILE)
+        tokens = xs_all[:, :, cols].reshape(16 * ROWS, TILE)
+        ga_ref[:, cols] = scale * dot_nn(lg_t[...], tokens)
+        return carry
+
+    lax.fori_loop(0, D_LOCAL // TILE, ga_body, 0)
+
     low_rows = lg[wi]
 
     def ig_body(t, carry):
@@ -458,22 +474,10 @@
         ig_ref[:, cols] = (base + ADAPTER_SCALE * dot_nt(low_rows, a[cols, :])).astype(BF16)
         return carry
 
-    lax.fori_loop(0, D_LOCAL // TILE, ig_body, 0)
-
-    spread_end(xs_all, in_ss, in_rs)
-    for xl_ in (0, 1):
-        for y_ in range(4):
-            other = wide_id(xl_, y_, 1 - c)
-            arrived(lg.at[other], lg_rs.at[other], lg_ss.at[0])
-    lg_t[...] = lg[...].reshape(16 * ROWS, R).T
-
-    def ga_body(t, carry):
-        cols = pl.ds(pl.multiple_of(t * TILE, TILE), TILE)
-        tokens = xs_all[:, :, cols].reshape(16 * ROWS, TILE)
-        ga_ref[:, cols] = scale * dot_nn(lg_t[...], tokens)
-        return carry
-
-    lax.fori_loop(0, D_LOCAL // TILE, ga_body, 0)
+    for part in range(PARTS):
+        if part:
+            arrived(x_recv.at[part], x_rs.at[part], x_ss.at[part])
+        lax.fori_loop(max(part * PER_PART - 1, 0), (part + 1) * PER_PART - 1, ig_body, 0)
 
     for sem, cut in enumerate(g_sends):
         sent(g_slot((0, 0), None)[0] if cut is None else g.at[0, pl.ds(*CUTS[cut])], g_ss.at[sem], g_rs.at[0])

time: 152 us -> 146 us (0.961); the launches traced: 151 us -> 143 us
  Pallas kernels: 144 us -> 136 us
    pallas_call x1, Pallas kernels: 144 us -> 136 us  [shards(): pl.pallas_call(kernel, out_shape=(jax.ShapeDtypeStruct((ROWS, D_LOCAL), B...]
where the time goes in v3:
time: 146 us; the launch traced here: 143 us
  Pallas kernels  136 us (93%)
  local copies, waits for them, and re-layouts  6.61 us (5%)
    pallas_call x1, Pallas kernels, shards(): pl.pallas_call(kernel, out_shape=(jax.ShapeDtypeStruct((ROWS, D_LOCAL), B...  136 us
    unnamed x5, local copies, waits for them, and re-layouts  6.61 us

profile of v3, /device:TPU:2, one launch (start us, length us, event | category | flops | bytes accessed | tf_op | source)
XLA Modules:
  0.0 143.4 jit_solution(4655691240282066299)
XLA Ops:
  0.6 136.1 %backward.1 = (bf16[112,2048]{1,0:T(8,128)(2,1)}, f32[256,2048]{1,0:T(8,128)}, f32[256,3328]{1,0:T(8,128)}) custom-call(bf16[112,2048]{1,0:T(8,128)(2,1)} %x_hbm.1, bf16[224,3328]{1,0:T(8,128)(2,1)} %g_hbm.1, bf16[2048,3328]{1,0:T(8,128)(2,1)} %w_hbm.1, bf16[2048,256]{1,0:T(8,128)(2,1)} %a_hbm.1, bf16[256,3328]{1,0:T(8,128)(2,1)} %b_hbm.1), custom_call_target="tpu_custom_call" | custom-call | tf_op jit(solution)/shard_map/backward/pallas_call | solution.py:541
  136.8 0.0 copy-start
  136.8 3.0 %copy.8 = f32[2048,256]{1,0:T(8,128)} copy(f32[2048,256]{0,1:T(8,128)} %bitcast.1) | data formatting | bytes 4194304
  139.8 1.8 %copy.11 = bf16[112,2048]{1,0:T(8,128)(2,1)} copy(bf16[112,2048]{1,0:T(8,128)(2,1)} %get-tuple-element.15) | data formatting | bytes 917504
  141.6 0.0 copy-done
  141.6 1.8 %copy.12 = f32[256,3328]{1,0:T(8,128)} copy(f32[256,3328]{1,0:T(8,128)S(1)} %copy-done) | data formatting | bytes 6815744
Async XLA Ops:
  136.8 4.9 %copy-start = (f32[256,3328]{1,0:T(8,128)S(1)}, f32[256,3328]{1,0:T(8,128)}, u32[]{:S(2)}) copy-start(f32[256,3328]{1,0:T(8,128)} %get-tuple-element.17) | copy-start | bytes 10223620

commit v4 on v3

--- a/solution.py
+++ b/solution.py
@@ -49,10 +49,11 @@
 
 def kernel(
     x_hbm, g_hbm, w_hbm, a_hbm, b_hbm,
+    ig_hbm, ga_hbm, gb_hbm,
     ig_ref, ga_ref, gb_ref,
     g, w, a, xs_all, part_send, part_recv, mine, relay, y_recv, y_own, x_send, x_recv,
     lp, l1, l2s, l2r, lo, la, la_t, lg, lg_t,
-    ld_sem, g_ss, g_rs, c_ss, c_rs, f_rs, y_ss, y_rs, x_ss, x_rs,
+    ld_sem, out_sem, g_ss, g_rs, c_ss, c_rs, f_rs, y_ss, y_rs, x_ss, x_rs,
     in_ss, in_rs, la_ss, la_rs, lg_ss, lg_rs, l1_ss, l1_rs, l2_ss, l2_rs, l3_ss, l3_rs,
 ):
     wi = lax.axis_index("wide")
@@ -169,10 +170,6 @@
                 other = wide_id(xl_, y_, 1 - c)
                 arrived(buf.at[other], rs.at[other], ss.at[0])
 
-    def spread_sent(buf, ss, rs):
-        for i in range(15):
-            sent(buf.at[wi], ss.at[i], rs.at[wi])
-
     loads[0].wait()
     spread_own(xs_all, in_ss, in_rs)
 
@@ -328,6 +325,40 @@
                 send(me, me, lg_ss.at[1 + i], lg_rs.at[wi], wide_dev((xl + dx) % 2, ring(y, k), c))
 
         return 0
+
+    def drain(step, carry):
+        xl_n, y_n = owner(step)
+        for part in range(PARTS):
+            sent(part_send.at[step, part], c_ss.at[step, part], c_rs.at[step, part])
+
+        @pl.when(y_n != y)
+        def _():
+            for part in range(PARTS):
+                for h in (0, 1):
+                    sent(part_recv.at[step, part, h], y_ss.at[step, part, h], y_rs.at[0, 0, part, h])
+
+        return carry
+
+    def drain_first():
+        for sem in range(5):
+            sent(g.at[0], g_ss.at[sem], g_rs.at[0])
+        for k in range(3):
+            sent(lp.at[0], l1_ss.at[k], l1_rs.at[k])
+            sent(lo.at[0], l3_ss.at[k], l3_rs.at[k])
+        sent(l2s, l2_ss, l2_rs)
+        for i in range(5):
+            sent(xs_all.at[wi], in_ss.at[i], in_rs.at[wi])
+        lax.fori_loop(0, 2, drain, 0)
+
+    def drain_most():
+        for sem, cut in enumerate(g_sends):
+            if sem >= 5:
+                sent(g.at[0] if cut is None else g.at[0, pl.ds(*CUTS[cut])], g_ss.at[sem], g_rs.at[0])
+        for i in range(15):
+            sent(la.at[wi], la_ss.at[i], la_rs.at[wi])
+            if i >= 5:
+                sent(xs_all.at[wi], in_ss.at[i], in_rs.at[wi])
+        lax.fori_loop(2, 6, drain, 0)
 
     def before(step):
         if step == 1:
@@ -361,6 +392,7 @@
             spread_core(xs_all, in_ss, in_rs, range(3))
             join_y_all(0)
             join_y_all(1)
+            drain_first()
             g_wait(6, 1, 0)
             g_send((6, 1), (7, 1), z_next, 0)
             g_wait(5, 0)
@@ -443,8 +475,11 @@
         return carry
 
     lax.fori_loop(0, F_LOCAL // TILE, gb_body, 0)
+    gb_out = pltpu.make_async_copy(gb_ref, gb_hbm, out_sem.at[0])
+    gb_out.start()
 
     announce_all(6)
+    drain_most()
     join_y_all(7)
     announce_all(7)
     for i, (dx, k) in enumerate(CHIPS):
@@ -460,7 +495,8 @@
     def ga_body(t, carry):
         cols = pl.ds(pl.multiple_of(t * TILE, TILE), TILE)
         tokens = xs_all[:, :, cols].reshape(16 * ROWS, TILE)
-        ga_ref[:, cols] = scale * dot_nn(lg_t[...], tokens)
+        ga_ref[t] = scale * dot_nn(lg_t[...], tokens)
+        pltpu.make_async_copy(ga_ref.at[t], ga_hbm.at[t], out_sem.at[2 + t]).start()
         return carry
 
     lax.fori_loop(0, D_LOCAL // TILE, ga_body, 0)
@@ -479,37 +515,48 @@
             arrived(x_recv.at[part], x_rs.at[part], x_ss.at[part])
         lax.fori_loop(max(part * PER_PART - 1, 0), (part + 1) * PER_PART - 1, ig_body, 0)
 
-    for sem, cut in enumerate(g_sends):
-        sent(g_slot((0, 0), None)[0] if cut is None else g.at[0, pl.ds(*CUTS[cut])], g_ss.at[sem], g_rs.at[0])
-    for k in range(3):
-        sent(lp.at[0], l1_ss.at[k], l1_rs.at[k])
-        sent(lo.at[0], l3_ss.at[k], l3_rs.at[k])
-    sent(l2s, l2_ss, l2_rs)
-    spread_sent(xs_all, in_ss, in_rs)
-    spread_sent(la, la_ss, la_rs)
-    spread_sent(lg, lg_ss, lg_rs)
-
-    def drain(step, carry):
-        xl_n, y_n = owner(step)
-        for part in range(PARTS):
-            sent(part_send.at[step, part], c_ss.at[step, part], c_rs.at[step, part])
-
-            @pl.when(y_n != y)
-            def _(part=part):
-                for h in (0, 1):
-                    sent(part_recv.at[step, part, h], y_ss.at[step, part, h], y_rs.at[0, 0, part, h])
-
-        return carry
-
-    lax.fori_loop(0, STEPS, drain, 0)
+    ig_out = pltpu.make_async_copy(ig_ref, ig_hbm, out_sem.at[1])
+    ig_out.start()
+
+    for i in range(15):
+        sent(lg.at[wi], lg_ss.at[i], lg_rs.at[wi])
+    lax.fori_loop(6, STEPS, drain, 0)
+    gb_out.wait()
+    for t in range(D_LOCAL // TILE):
+        pltpu.make_async_copy(ga_ref.at[t], ga_hbm.at[t], out_sem.at[2 + t]).wait()
+    ig_out.wait()
     for part in range(PARTS):
         sent(x_send.at[part], x_ss.at[part], x_rs.at[part])
+
+
+def results(ig, ga, gb, ig_out, ga_out, gb_out, ig_buf, ga_buf, gat_buf, gb_buf, in_sem, out_sem):
+    blocks = D_LOCAL // TILE
+    rows = R // 4
+    pairs = [(ga.at[t], ga_buf.at[t], gat_buf.at[t], ga_out.at[pl.ds(t * TILE, TILE)]) for t in range(blocks)]
+    for i in range(4):
+        cut = pl.ds(i * rows, rows)
+        pairs.append((gb.at[cut], gb_buf.at[cut], gb_buf.at[cut], gb_out.at[cut]))
+    pairs.append((ig, ig_buf, ig_buf, ig_out))
+    loads = [pltpu.make_async_copy(p[0], p[1], in_sem.at[i]) for i, p in enumerate(pairs)]
+    stores = [pltpu.make_async_copy(p[2], p[3], out_sem.at[i]) for i, p in enumerate(pairs)]
+    for cp in loads:
+        cp.start()
+    for i in range(len(pairs)):
+        loads[i].wait()
+        if i < blocks:
+            gat_buf[i] = ga_buf[i].T
+        stores[i].start()
+    for cp in stores:
+        cp.wait()
 
 
 def shards(inputs, grad_out, w_base, adapter_down_matrix, b_factor):
     dma = pltpu.SemaphoreType.DMA
     pieces = (PARTS, 2, PER_PART, ROWS, HALF)
     scratch = [
+        pltpu.VMEM((ROWS, D_LOCAL), BF16),
+        pltpu.VMEM((D_LOCAL // TILE, R, TILE), F32),
+        pltpu.VMEM((R, F_LOCAL), F32),
         pltpu.VMEM((16, ROWS, F_LOCAL), BF16),
         pltpu.VMEM((R + D_LOCAL, F_LOCAL), BF16),
         pltpu.VMEM((D_LOCAL, R), BF16),
@@ -531,29 +578,47 @@
         pltpu.VMEM((16 * ROWS, R), BF16),
         pltpu.VMEM((16, ROWS, R), BF16),
         pltpu.VMEM((R, 16 * ROWS), BF16),
-        dma((6,)), dma((16,)), dma((18,)), dma((STEPS, PARTS)), dma((STEPS, PARTS)),
+        dma((6,)), dma((10,)), dma((16,)), dma((18,)), dma((STEPS, PARTS)), dma((STEPS, PARTS)),
         dma((2, 2, PARTS)), dma((STEPS, PARTS, 2)), dma((2, 2, PARTS, 2)), dma((PARTS,)), dma((PARTS,)),
         dma((15,)), dma((16,)), dma((15,)), dma((16,)), dma((15,)), dma((16,)),
         dma((3,)), dma((3,)), dma(()), dma(()), dma((3,)), dma((4,)),
     ]
     any_spec = pl.BlockSpec(memory_space=pl.ANY)
-    vmem_spec = pl.BlockSpec(memory_space=pltpu.VMEM)
     input_gradient, grad_a, grad_b = pl.pallas_call(
         kernel,
         out_shape=(
             jax.ShapeDtypeStruct((ROWS, D_LOCAL), BF16),
-            jax.ShapeDtypeStruct((R, D_LOCAL), F32),
+            jax.ShapeDtypeStruct((D_LOCAL // TILE, R, TILE), F32),
             jax.ShapeDtypeStruct((R, F_LOCAL), F32),
         ),
         in_specs=[any_spec] * 5,
-        out_specs=(vmem_spec,) * 3,
+        out_specs=(any_spec,) * 3,
         scratch_shapes=scratch,
         compiler_params=pltpu.CompilerParams(
             collective_id=0, has_side_effects=True, vmem_limit_bytes=67043328
         ),
         name="backward",
     )(inputs, grad_out, w_base, adapter_down_matrix, b_factor)
-    return input_gradient, grad_a.T, grad_b
+    blocks = D_LOCAL // TILE
+    return pl.pallas_call(
+        results,
+        out_shape=(
+            jax.ShapeDtypeStruct((ROWS, D_LOCAL), BF16),
+            jax.ShapeDtypeStruct((D_LOCAL, R), F32),
+            jax.ShapeDtypeStruct((R, F_LOCAL), F32),
+        ),
+        in_specs=[any_spec] * 3,
+        out_specs=(any_spec,) * 3,
+        scratch_shapes=[
+            pltpu.VMEM((ROWS, D_LOCAL), BF16),
+            pltpu.VMEM((blocks, R, TILE), F32),
+            pltpu.VMEM((blocks, TILE, R), F32),
+            pltpu.VMEM((R, F_LOCAL), F32),
+            dma((blocks + 5,)),
+            dma((blocks + 5,)),
+        ],
+        name="results",
+    )(input_gradient, grad_a, grad_b)
 
 
 def solution(mesh):

time: 146 us -> 143 us (0.979)
  local copies, waits for them, and re-layouts: 6.61 us -> 0 us
  Pallas kernels: 136 us -> 139 us
    unnamed x5 -> x0, local copies, waits for them, and re-layouts: 6.61 us -> none
    pallas_call x0 -> x1, Pallas kernels: none -> 5.3 us  [shards(): pl.pallas_call(results, out_shape=(jax.ShapeDtypeStruct((ROWS, D_LOCAL),...]
    pallas_call x1, Pallas kernels: 136 us -> 134 us  [shards(): pl.pallas_call(kernel, out_shape=(jax.ShapeDtypeStruct((ROWS, D_LOCAL), B...]
where the time goes in v4:
time: 143 us; the launch traced here: 140 us
  Pallas kernels  139 us (97%)
    pallas_call x1, Pallas kernels, shards(): pl.pallas_call(kernel, out_shape=(jax.ShapeDtypeStruct((ROWS, D_LOCAL), B...  134 us
    pallas_call x1, Pallas kernels, shards(): pl.pallas_call(results, out_shape=(jax.ShapeDtypeStruct((ROWS, D_LOCAL),...  5.3 us

profile of v4, /device:TPU:2, one launch (start us, length us, event | category | flops | bytes accessed | tf_op | source)
XLA Modules:
  0.0 140.1 jit_solution(15526372088620248165)
XLA Ops:
  0.6 134.2 %backward.1 = (bf16[112,2048]{1,0:T(8,128)(2,1)}, f32[8,256,256]{2,1,0:T(8,128)}, f32[256,3328]{1,0:T(8,128)}) custom-call(bf16[112,2048]{1,0:T(8,128)(2,1)} %x_hbm.1, bf16[224,3328]{1,0:T(8,128)(2,1)} %g_hbm.1, bf16[2048,3328]{1,0:T(8,128)(2,1)} %w_hbm.1, bf16[2048,256]{1,0:T(8,128)(2,1)} %a_hbm.1, bf16[256,3328]{1,0:T(8,128)(2,1)} %b_hbm.1), custom_call_target="tpu_custom_call" | custom-call | tf_op jit(solution)/shard_map/backward/pallas_call | solution.py:587
  134.8 5.3 %results.1 = (bf16[112,2048]{1,0:T(8,128)(2,1)}, f32[2048,256]{1,0:T(8,128)}, f32[256,3328]{1,0:T(8,128)}) custom-call(bf16[112,2048]{1,0:T(8,128)(2,1)} %get-tuple-element.6.ig, f32[8,256,256]{2,1,0:T(8,128)} %get-tuple-element.7.ga, f32[256,3328]{1,0:T(8,128)} %get-tuple-element.8.gb), custom_call_target="tpu_custom_call" | custom-call | tf_op jit(solution)/shard_map/results/pallas_call | solution.py:603

commit v5 on v4

--- a/solution.py
+++ b/solution.py
@@ -480,13 +480,32 @@
 
     announce_all(6)
     drain_most()
-    join_y_all(7)
+    join_y(7, 0)
     announce_all(7)
+    join_y(7, 1)
+    join_y(7, 2)
     for i, (dx, k) in enumerate(CHIPS):
         other = wide_id((xl + dx) % 2, ring(y, k), c)
         blk = lg.at[other]
         arrived(blk, lg_rs.at[other], lg_ss.at[0])
         send(blk, blk, lg_ss.at[8 + i], lg_rs.at[other], partner)
+
+    low_rows = lg[wi]
+
+    def ig_body(t, carry):
+        cols = pl.ds(pl.multiple_of(t * TILE, TILE), TILE)
+        part, i = (t + 1) // PER_PART, (t + 1) % PER_PART
+        base = jnp.concatenate([own_total(part, 0, i), own_total(part, 1, i)], axis=1)
+        ig_ref[:, cols] = (base + ADAPTER_SCALE * dot_nt(low_rows, a[cols, :])).astype(BF16)
+        return carry
+
+    def ig_part(part):
+        if part:
+            arrived(x_recv.at[part], x_rs.at[part], x_ss.at[part])
+        lax.fori_loop(max(part * PER_PART - 1, 0), (part + 1) * PER_PART - 1, ig_body, 0)
+
+    ig_part(0)
+    ig_part(1)
 
     spread_end(xs_all, in_ss, in_rs)
     spread_end(lg, lg_ss, lg_rs)
@@ -501,20 +520,7 @@
 
     lax.fori_loop(0, D_LOCAL // TILE, ga_body, 0)
 
-    low_rows = lg[wi]
-
-    def ig_body(t, carry):
-        cols = pl.ds(pl.multiple_of(t * TILE, TILE), TILE)
-        part, i = (t + 1) // PER_PART, (t + 1) % PER_PART
-        base = jnp.concatenate([own_total(part, 0, i), own_total(part, 1, i)], axis=1)
-        ig_ref[:, cols] = (base + ADAPTER_SCALE * dot_nt(low_rows, a[cols, :])).astype(BF16)
-        return carry
-
-    for part in range(PARTS):
-        if part:
-            arrived(x_recv.at[part], x_rs.at[part], x_ss.at[part])
-        lax.fori_loop(max(part * PER_PART - 1, 0), (part + 1) * PER_PART - 1, ig_body, 0)
-
+    ig_part(2)
     ig_out = pltpu.make_async_copy(ig_ref, ig_hbm, out_sem.at[1])
     ig_out.start()
 

time: 143 us -> 142 us (level)
  no operation moved by 1% of the time
where the time goes in v5:
time: 142 us; the launch traced here: 140 us
  Pallas kernels  140 us (99%)
    pallas_call x1, Pallas kernels, shards(): pl.pallas_call(kernel, out_shape=(jax.ShapeDtypeStruct((ROWS, D_LOCAL), B...  134 us
    pallas_call x1, Pallas kernels, shards(): pl.pallas_call(results, out_shape=(jax.ShapeDtypeStruct((ROWS, D_LOCAL),...  5.3 us

profile of v5, /device:TPU:2, one launch (start us, length us, event | category | flops | bytes accessed | tf_op | source)
XLA Modules:
  0.0 140.1 jit_solution(393867575191050990)
XLA Ops:
  0.6 134.2 %backward.1 = (bf16[112,2048]{1,0:T(8,128)(2,1)}, f32[8,256,256]{2,1,0:T(8,128)}, f32[256,3328]{1,0:T(8,128)}) custom-call(bf16[112,2048]{1,0:T(8,128)(2,1)} %x_hbm.1, bf16[224,3328]{1,0:T(8,128)(2,1)} %g_hbm.1, bf16[2048,3328]{1,0:T(8,128)(2,1)} %w_hbm.1, bf16[2048,256]{1,0:T(8,128)(2,1)} %a_hbm.1, bf16[256,3328]{1,0:T(8,128)(2,1)} %b_hbm.1), custom_call_target="tpu_custom_call" | custom-call | tf_op jit(solution)/shard_map/backward/pallas_call | solution.py:593
  134.8 5.3 %results.1 = (bf16[112,2048]{1,0:T(8,128)(2,1)}, f32[2048,256]{1,0:T(8,128)}, f32[256,3328]{1,0:T(8,128)}) custom-call(bf16[112,2048]{1,0:T(8,128)(2,1)} %get-tuple-element.6.ig, f32[8,256,256]{2,1,0:T(8,128)} %get-tuple-element.7.ga, f32[256,3328]{1,0:T(8,128)} %get-tuple-element.8.gb), custom_call_target="tpu_custom_call" | custom-call | tf_op jit(solution)/shard_map/results/pallas_call | solution.py:609

commit v6 on v5

--- a/solution.py
+++ b/solution.py
@@ -53,7 +53,7 @@
     ig_ref, ga_ref, gb_ref,
     g, w, a, xs_all, part_send, part_recv, mine, relay, y_recv, y_own, x_send, x_recv,
     lp, l1, l2s, l2r, lo, la, la_t, lg, lg_t,
-    ld_sem, out_sem, g_ss, g_rs, c_ss, c_rs, f_rs, y_ss, y_rs, x_ss, x_rs,
+    ld_sem, out_sem, ig_sem, g_ss, g_rs, c_ss, c_rs, f_rs, y_ss, y_rs, x_ss, x_rs,
     in_ss, in_rs, la_ss, la_rs, lg_ss, lg_rs, l1_ss, l1_rs, l2_ss, l2_rs, l3_ss, l3_rs,
 ):
     wi = lax.axis_index("wide")
@@ -496,7 +496,8 @@
         cols = pl.ds(pl.multiple_of(t * TILE, TILE), TILE)
         part, i = (t + 1) // PER_PART, (t + 1) % PER_PART
         base = jnp.concatenate([own_total(part, 0, i), own_total(part, 1, i)], axis=1)
-        ig_ref[:, cols] = (base + ADAPTER_SCALE * dot_nt(low_rows, a[cols, :])).astype(BF16)
+        ig_ref[t] = (base + ADAPTER_SCALE * dot_nt(low_rows, a[cols, :])).astype(BF16)
+        pltpu.make_async_copy(ig_ref.at[t], ig_hbm.at[:, cols], ig_sem.at[t]).start()
         return carry
 
     def ig_part(part):
@@ -521,16 +522,15 @@
     lax.fori_loop(0, D_LOCAL // TILE, ga_body, 0)
 
     ig_part(2)
-    ig_out = pltpu.make_async_copy(ig_ref, ig_hbm, out_sem.at[1])
-    ig_out.start()
-
     for i in range(15):
         sent(lg.at[wi], lg_ss.at[i], lg_rs.at[wi])
     lax.fori_loop(6, STEPS, drain, 0)
     gb_out.wait()
     for t in range(D_LOCAL // TILE):
         pltpu.make_async_copy(ga_ref.at[t], ga_hbm.at[t], out_sem.at[2 + t]).wait()
-    ig_out.wait()
+    for t in range(D_LOCAL // TILE):
+        cols = pl.ds(t * TILE, TILE)
+        pltpu.make_async_copy(ig_ref.at[t], ig_hbm.at[:, cols], ig_sem.at[t]).wait()
     for part in range(PARTS):
         sent(x_send.at[part], x_ss.at[part], x_rs.at[part])
 
@@ -560,7 +560,7 @@
     dma = pltpu.SemaphoreType.DMA
     pieces = (PARTS, 2, PER_PART, ROWS, HALF)
     scratch = [
-        pltpu.VMEM((ROWS, D_LOCAL), BF16),
+        pltpu.VMEM((D_LOCAL // TILE, ROWS, TILE), BF16),
         pltpu.VMEM((D_LOCAL // TILE, R, TILE), F32),
         pltpu.VMEM((R, F_LOCAL), F32),
         pltpu.VMEM((16, ROWS, F_LOCAL), BF16),
@@ -584,7 +584,7 @@
         pltpu.VMEM((16 * ROWS, R), BF16),
         pltpu.VMEM((16, ROWS, R), BF16),
         pltpu.VMEM((R, 16 * ROWS), BF16),
-        dma((6,)), dma((10,)), dma((16,)), dma((18,)), dma((STEPS, PARTS)), dma((STEPS, PARTS)),
+        dma((6,)), dma((10,)), dma((8,)), dma((16,)), dma((18,)), dma((STEPS, PARTS)), dma((STEPS, PARTS)),
         dma((2, 2, PARTS)), dma((STEPS, PARTS, 2)), dma((2, 2, PARTS, 2)), dma((PARTS,)), dma((PARTS,)),
         dma((15,)), dma((16,)), dma((15,)), dma((16,)), dma((15,)), dma((16,)),
         dma((3,)), dma((3,)), dma(()), dma(()), dma((3,)), dma((4,)),

time: 142 us -> 142 us (level)
  no operation moved by 1% of the time
where the time goes in v6:
time: 142 us; the launch traced here: 140 us
  Pallas kernels  139 us (98%)
    pallas_call x1, Pallas kernels, shards(): pl.pallas_call(kernel, out_shape=(jax.ShapeDtypeStruct((ROWS, D_LOCAL), B...  134 us
    pallas_call x1, Pallas kernels, shards(): pl.pallas_call(results, out_shape=(jax.ShapeDtypeStruct((ROWS, D_LOCAL),...  5.3 us

profile of v6, /device:TPU:2, one launch (start us, length us, event | category | flops | bytes accessed | tf_op | source)
XLA Modules:
  0.0 140.0 jit_solution(4763930269167653876)
XLA Ops:
  0.6 134.1 %backward.1 = (bf16[112,2048]{1,0:T(8,128)(2,1)}, f32[8,256,256]{2,1,0:T(8,128)}, f32[256,3328]{1,0:T(8,128)}) custom-call(bf16[112,2048]{1,0:T(8,128)(2,1)} %x_hbm.1, bf16[224,3328]{1,0:T(8,128)(2,1)} %g_hbm.1, bf16[2048,3328]{1,0:T(8,128)(2,1)} %w_hbm.1, bf16[2048,256]{1,0:T(8,128)(2,1)} %a_hbm.1, bf16[256,3328]{1,0:T(8,128)(2,1)} %b_hbm.1), custom_call_target="tpu_custom_call" | custom-call | tf_op jit(solution)/shard_map/backward/pallas_call | solution.py:593
  134.7 5.3 %results.1 = (bf16[112,2048]{1,0:T(8,128)(2,1)}, f32[2048,256]{1,0:T(8,128)}, f32[256,3328]{1,0:T(8,128)}) custom-call(bf16[112,2048]{1,0:T(8,128)(2,1)} %get-tuple-element.6.ig, f32[8,256,256]{2,1,0:T(8,128)} %get-tuple-element.7.ga, f32[256,3328]{1,0:T(8,128)} %get-tuple-element.8.gb), custom_call_target="tpu_custom_call" | custom-call | tf_op jit(solution)/shard_map/results/pallas_call | solution.py:609
